TPU v7x, 256 devices: a whole 4x4x8 slice. The times are simulated.
256 devices in a mesh: req: 64 (over z, x, core), tp: 4 (over y).
Axes of the slice: x: 4, y: 4, z: 8, core: 2. Of those that a mesh axis runs over, the one named last changes fastest.
Arguments:
- hidden_in: bfloat16 [32768, 1024], P('req', 'tp'), may hold values from -6 to 6
- w_qkv: bfloat16 [1024, 3, 1024], P(None, None, 'tp'), may hold values from -0.1875 to 0.1875
- w_out: bfloat16 [1024, 1024], P('tp'), may hold values from -0.75 to 0.75
- first_gain: float32 [1024], replicated, may hold values from 0.1 to 1.9
- w_up: bfloat16 [1024, 4096], P(None, 'tp'), may hold values from -0.1875 to 0.1875
- w_down: bfloat16 [4096, 1024], P('tp'), may hold values from -0.09375 to 0.09375
- second_gain: float32 [1024], replicated, may hold values from 0.1 to 1.9
- cache_pool: bfloat16 [4096, 128, 2, 1024], P('req', None, None, 'tp'), may hold values from -600 to 600
- page_table: int32 [512, 8], P('req'), may hold values from 0 to 63, as said below
- cache_len: int32 [512], P('req'), may hold values from 1 to 1024, as said below
- tree_parent: int32 [512, 64], P('req'), may hold values from -1 to 62, as said below
- accept_node: int32 [512], P('req'), may hold values from 0 to 63
Outputs:
- layer_out: bfloat16 [32768, 1024], P('req', 'tp')
- accepted_kv: bfloat16 [512, 64, 2, 1024], P('req', None, None, 'tp')
Inputs may be any that keep to these rules, and one draw needn't show every extreme that they name: `page_table`: on each index e of req, the 8 x 8 entries of its rows are a permutation of the slots 0 to 63; row j, column m holds the slot in e's pool of page j of member m of the index e - j of req (modulo the axis size). `cache_len`: on each index of req exactly 2 requests have lengths over 256, and the others at most 256; the length 1024 occurs in every draw, and so does the length 256. `tree_parent`: node 0 is the root with parent -1; every other node's parent is an earlier node.
All inputs are finite; a program needn't handle non-finite values.
Results may differ from a plain program's by a relative error of at most 0.012.
Values may be sent and summed in bfloat16 or wider, within the bound.
A program may use at most 128 MiB of HBM per device.

v0:
```python
import jax
import jax.numpy as jnp
from jax import lax
from jax.sharding import PartitionSpec as P

HD = 64
NEG = -1e30
EPS = 1e-05


def from_behind(value, axis, by):
    size = lax.axis_size(axis)
    return lax.ppermute(value, axis, [(i, (i + by) % size) for i in range(size)])


def block_partial(queries, key_rows, value_rows, valid):
    scores = jnp.einsum("bqhd,bkhd->bhqk", queries, key_rows, preferred_element_type=jnp.float32)
    allowed = valid[:, None, :, :]
    maxima = jnp.max(jnp.where(allowed, scores, NEG), axis=-1)
    weights = jnp.where(allowed, jnp.exp(scores - maxima[..., None]), 0.0).astype(jnp.bfloat16)
    totals = jnp.sum(weights.astype(jnp.float32), axis=-1)
    mixture = jnp.einsum("bhqk,bkhd->bqhd", weights, value_rows, preferred_element_type=jnp.float32)
    return (mixture, maxima, totals)


def combine_blocks(mixture, maxima, totals):
    best = jnp.max(maxima, axis=0)
    scale = jnp.swapaxes(jnp.exp(maxima - best[None]), -1, -2)
    numer = jnp.sum(mixture * scale[..., None], axis=0)
    denom = jnp.sum(jnp.swapaxes(totals, -1, -2) * scale, axis=0)
    return numer / denom[..., None]


def ancestors(parents):
    count = parents.shape[-1]
    reach = jax.nn.one_hot(parents, count, dtype=jnp.float32) + jnp.eye(count, dtype=jnp.float32)
    for sweep in range(max(1, (count - 1).bit_length())):
        reach = jnp.minimum(
            jnp.einsum("rij,rjk->rik", reach, reach, precision=lax.Precision.HIGHEST), 1.0
        )
    return reach


def page_rows(cache_pool, slot_ids):
    picker = jax.nn.one_hot(slot_ids, cache_pool.shape[0], dtype=jnp.bfloat16)
    return jnp.einsum(
        "rs,spcf->rpcf", picker, cache_pool, preferred_element_type=jnp.float32
    ).astype(jnp.bfloat16)


def rows_split(rows, heads_local):
    requests, page_len = (rows.shape[0], rows.shape[1])
    return (
        rows[:, :, 0].reshape(requests, page_len, heads_local, HD),
        rows[:, :, 1].reshape(requests, page_len, heads_local, HD),
    )


def page_split(cache_pool, slot_ids, heads_local):
    return rows_split(page_rows(cache_pool, slot_ids), heads_local)


def spread_back(arrived, long_ids, requests):
    mixture = (
        jnp.zeros((requests,) + arrived[0].shape[1:], jnp.float32).at[long_ids].set(arrived[0])
    )
    maxima = (
        jnp.full((requests,) + arrived[1].shape[1:], NEG, jnp.float32).at[long_ids].set(arrived[1])
    )
    totals = jnp.zeros((requests,) + arrived[2].shape[1:], jnp.float32).at[long_ids].set(arrived[2])
    return (mixture, maxima, totals)


def norm_from_sums(values, sums, gain, width_all):
    center = (sums[0] / width_all)[:, None]
    spread = (sums[1] / width_all)[:, None] - center * center
    return (values - center) * lax.rsqrt(spread + EPS) * gain


def shards(
    hidden_in,
    w_qkv,
    w_out,
    first_gain,
    w_up,
    w_down,
    second_gain,
    cache_pool,
    page_table,
    cache_len,
    tree_parent,
    accept_node,
):
    tokens_dev, share = hidden_in.shape
    requests, draft = tree_parent.shape
    width_local = w_qkv.shape[2]
    heads_local = width_local // HD
    page_count = page_table.shape[0]
    page_len = cache_pool.shape[1]
    width_all = share * lax.axis_size("tp")
    start = lax.axis_index("tp") * share
    gathered = lax.all_gather(hidden_in, "tp", axis=1, tiled=True)
    projected = jnp.einsum("td,dcf->tcf", gathered, w_qkv, preferred_element_type=jnp.float32)
    queries = (
        (projected[:, 0] * 0.125).astype(jnp.bfloat16).reshape(requests, draft, heads_local, HD)
    )
    key_new = projected[:, 1].astype(jnp.bfloat16)
    value_new = projected[:, 2].astype(jnp.bfloat16)
    key_heads = key_new.reshape(requests, draft, heads_local, HD)
    value_heads = value_new.reshape(requests, draft, heads_local, HD)
    reach = ancestors(tree_parent)
    long_count = (requests + 3) // 4
    is_long = (cache_len > 2 * page_len).astype(jnp.int32)
    rank_score = is_long * (2 * requests) + (requests - jnp.arange(requests, dtype=jnp.int32))
    ranked, long_ids = lax.top_k(rank_score, long_count)
    long_queries = queries[long_ids]
    member_code = long_ids.astype(jnp.bfloat16)
    parts = [block_partial(queries, key_heads, value_heads, reach > 0.5)]
    positions = jnp.arange(page_len, dtype=jnp.int32)
    for page_index in range(page_count):
        valid_rows = page_index * page_len + positions[None, :] < cache_len[:, None]
        valid = jnp.broadcast_to(valid_rows[:, None, :], (requests, draft, page_len))
        if page_index == 0:
            key_rows, value_rows = page_split(cache_pool, page_table[0], heads_local)
            result = block_partial(queries, key_rows, value_rows, valid)
        elif page_index == 1:
            incoming, flags = from_behind(
                (queries, valid_rows.astype(jnp.bfloat16)), "req", page_index
            )
            key_rows, value_rows = page_split(cache_pool, page_table[page_index], heads_local)
            remote_valid = jnp.broadcast_to((flags > 0.5)[:, None, :], (requests, draft, page_len))
            remote = block_partial(incoming, key_rows, value_rows, remote_valid)
            result = from_behind((remote[0], remote[1], remote[2]), "req", -page_index)
        else:
            long_flags = valid_rows[long_ids].astype(jnp.bfloat16)
            incoming, flags, members = from_behind(
                (long_queries, long_flags, member_code), "req", page_index
            )
            member_ids = members.astype(jnp.int32)
            key_rows, value_rows = page_split(
                cache_pool, page_table[page_index][member_ids], heads_local
            )
            remote_valid = jnp.broadcast_to(
                (flags > 0.5)[:, None, :], (long_count, draft, page_len)
            )
            remote = block_partial(incoming, key_rows, value_rows, remote_valid)
            arrived = from_behind((remote[0], remote[1], remote[2]), "req", -page_index)
            result = spread_back(arrived, long_ids, requests)
        parts.append(result)
    mixture = jnp.stack([piece[0] for piece in parts], axis=0)
    maxima = jnp.stack([piece[1] for piece in parts], axis=0)
    totals = jnp.stack([piece[2] for piece in parts], axis=0)
    attended = (
        combine_blocks(mixture, maxima, totals)
        .reshape(tokens_dev, width_local)
        .astype(jnp.bfloat16)
    )
    branch = jnp.dot(attended, w_out, preferred_element_type=jnp.float32)
    second_share = lax.dynamic_slice_in_dim(second_gain, start, share, 0)
    summed = lax.psum(branch, "tp")
    mixed_all = gathered.astype(jnp.float32) + summed
    whole_sums = (jnp.sum(mixed_all, axis=-1), jnp.sum(mixed_all * mixed_all, axis=-1))
    normed_all = norm_from_sums(mixed_all, whole_sums, first_gain, width_all).astype(jnp.bfloat16)
    normed_share = lax.dynamic_slice_in_dim(normed_all, start, share, 1)
    inner = jax.nn.gelu(
        jnp.dot(normed_all, w_up, preferred_element_type=jnp.float32), approximate=False
    ).astype(jnp.bfloat16)
    outer = lax.psum_scatter(
        jnp.dot(inner, w_down, preferred_element_type=jnp.float32).astype(jnp.bfloat16),
        "tp",
        scatter_dimension=1,
        tiled=True,
    ).astype(jnp.float32)
    second_in = normed_share.astype(jnp.float32) + outer
    second_sums = lax.psum(
        (jnp.sum(second_in, axis=-1), jnp.sum(second_in * second_in, axis=-1)), "tp"
    )
    layer_out = norm_from_sums(second_in, second_sums, second_share, width_all).astype(jnp.bfloat16)
    pairs = jnp.stack(
        [
            key_new.reshape(requests, draft, width_local),
            value_new.reshape(requests, draft, width_local),
        ],
        axis=2,
    )
    depth = jnp.sum(reach, axis=-1) - 1.0
    chosen = jnp.einsum(
        "rq,rqk->rk",
        jax.nn.one_hot(accept_node, draft, dtype=jnp.float32),
        reach,
        precision=lax.Precision.HIGHEST,
    )
    levels = jnp.arange(draft, dtype=jnp.float32)
    select = (
        chosen[:, None, :] * (depth[:, None, :] == levels[None, :, None]).astype(jnp.float32)
    ).astype(jnp.bfloat16)
    accepted_kv = jnp.einsum(
        "rsk,rkcf->rscf", select, pairs, preferred_element_type=jnp.float32
    ).astype(jnp.bfloat16)
    return (layer_out, accepted_kv)


def solution(mesh):
    placed = (
        P("req", "tp"),
        P(None, None, "tp"),
        P("tp", None),
        P(),
        P(None, "tp"),
        P("tp", None),
        P(),
        P("req", None, None, "tp"),
        P("req", None),
        P("req"),
        P("req", None),
        P("req"),
    )
    return jax.shard_map(
        shards,
        mesh=mesh,
        in_specs=placed,
        out_specs=(P("req", "tp"), P("req", None, None, "tp")),
        check_vma=False,
    )
```

profile of v0, /device:TPU:2, one launch (start us, length us, event | category | flops | bytes accessed | tf_op | source)
XLA Modules:
  0.0 424.8 jit_solution(16485412989436485535)
XLA Ops:
  11.1 4.3 %collective-permute-start.15 = (bf16[2]{0:T(256)(128)(2,1)S(1)}, bf16[2]{0:T(256)(128)(2,1)S(1)}, u32[]{:S(2)}, u32[]{:S(2)}) collective-permute-start(bf16[2]{0:T(256)(128)(2,1)S(1)} %get-tuple-element.60), channel_id=1, source_target_pairs={{0,20},{4,24},{8,28},{12,32},{16,36},{20,40},{24,44},{28,48},{32,5... | collective-permute-start | bytes 20 | tf_op jit(solution)/shard_map/ppermute | solution.py:13
  21.2 7.9 %convolution_convert_fusion.2 = bf16[8,128,2,256]{3,0,2,1:T(8,128)(2,1)S(1)} fusion(bf16[64,128,2,256]{3,2,1,0:T(2,128)(2,1)} %param.19, s32[8]{0:T(128)S(1)} %get-tuple-element.46), kind=kOutput, calls=%fused_computation.56 | convolution fusion | flops 67633664 | bytes 9437216 | tf_op jit(solution)/shard_map/rs,spcf->rpcf/dot_general | solution.py:46
  31.6 2.3 copy.165
  33.9 8.4 %convolution_convert_fusion.1 = bf16[8,128,2,256]{3,0,2,1:T(8,128)(2,1)S(1)} fusion(bf16[64,128,2,256]{3,2,1,0:T(2,128)(2,1)} %param.19, s32[8]{0:T(128)S(1)} %get-tuple-element.45), kind=kOutput, calls=%fused_computation.55 | convolution fusion | flops 67633664 | bytes 9437216 | tf_op jit(solution)/shard_map/rs,spcf->rpcf/dot_general | solution.py:46
  43.3 2.2 copy.168
  45.5 2.2 copy.170
  51.3 2.9 collective-permute-start.19
  55.3 8.0 %fusion.26 = bf16[2,128,2,256]{3,0,2,1:T(2,128)(2,1)S(1)} fusion(bf16[64,128,2,256]{3,2,1,0:T(2,128)(2,1)} %param.19, s32[2]{0:T(128)S(1)} %gather_fusion), kind=kOutput, calls=%fused_computation.77 | convolution fusion | flops 16908416 | bytes 8650760 | tf_op jit(solution)/shard_map/rs,spcf->rpcf/dot_general | solution.py:46
  64.8 8.0 %fusion.29 = bf16[2,128,2,256]{3,0,2,1:T(2,128)(2,1)S(1)} fusion(bf16[64,128,2,256]{3,2,1,0:T(2,128)(2,1)} %param.19, s32[2]{0:T(128)S(1)} %gather_fusion.3), kind=kOutput, calls=%fused_computation.78 | convolution fusion | flops 16908416 | bytes 8650760 | tf_op jit(solution)/shard_map/rs,spcf->rpcf/dot_general | solution.py:46
  73.7 2.4 collective-permute-start.4
  76.1 3.1 collective-permute-start.8
  79.9 8.0 %fusion.32 = bf16[2,128,2,256]{3,0,2,1:T(2,128)(2,1)S(1)} fusion(bf16[64,128,2,256]{3,2,1,0:T(2,128)(2,1)} %param.19, s32[2]{0:T(128)S(1)} %gather_fusion.5), kind=kOutput, calls=%fused_computation.79 | convolution fusion | flops 16908416 | bytes 8650760 | tf_op jit(solution)/shard_map/rs,spcf->rpcf/dot_general | solution.py:46
  89.4 8.0 %fusion.35 = bf16[2,128,2,256]{3,0,2,1:T(2,128)(2,1)S(1)} fusion(bf16[64,128,2,256]{3,2,1,0:T(2,128)(2,1)} %param.19, s32[2]{0:T(128)S(1)} %gather_fusion.7), kind=kOutput, calls=%fused_computation.80 | convolution fusion | flops 16908416 | bytes 8650760 | tf_op jit(solution)/shard_map/rs,spcf->rpcf/dot_general | solution.py:46
  98.3 2.0 collective-permute-start.12
  100.4 3.7 collective-permute-start.16
  104.7 8.0 %fusion.38 = bf16[2,128,2,256]{3,0,2,1:T(2,128)(2,1)S(1)} fusion(bf16[64,128,2,256]{3,2,1,0:T(2,128)(2,1)} %param.19, s32[2]{0:T(128)S(1)} %gather_fusion.9), kind=kOutput, calls=%fused_computation.81 | convolution fusion | flops 16908416 | bytes 8650760 | tf_op jit(solution)/shard_map/rs,spcf->rpcf/dot_general | solution.py:46
  114.2 8.0 %fusion.41 = bf16[2,128,2,256]{3,0,2,1:T(2,128)(2,1)S(1)} fusion(bf16[64,128,2,256]{3,2,1,0:T(2,128)(2,1)} %param.19, s32[2]{0:T(128)S(1)} %gather_fusion.11), kind=kOutput, calls=%fused_computation.82 | convolution fusion | flops 16908416 | bytes 8650760 | tf_op jit(solution)/shard_map/rs,spcf->rpcf/dot_general | solution.py:46
  138.8 1.8 collective-permute-start.24
  140.7 3.8 collective-permute-done.20
  144.5 2.7 fusion.45
  151.0 2.3 gather_fusion.2
  154.7 2.2 collective-permute-start.13
  159.1 2.0 convert_element_type.221
  161.1 2.0 convert_element_type.227
  172.9 2.1 collective-permute-start.35
  176.8 2.9 collective-permute-start.36
  182.2 3.0 collective-permute-start.37
  189.3 3.0 collective-permute-start.39
  193.5 4.2 collective-permute-start.29
  198.5 4.0 collective-permute-start.40
  204.2 3.1 collective-permute-start.32
  210.9 2.2 collective-permute-start.14
  213.4 4.9 %collective-permute-done.6 = f32[2,64,4,64]{1,3,2,0:T(8,128)S(1)} collective-permute-done((f32[2,64,4,64]{1,3,2,0:T(8,128)S(1)}, f32[2,64,4,64]{1,3,2,0:T(8,128)S(1)}, u32[]{:S(2)}, u32[]{:S(2)}) %collective-permute-start.6) | collective-permute-done | bytes 131104 | tf_op jit(solution)/shard_map/ppermute | solution.py:13
  218.3 4.8 %collective-permute-start.22 = (f32[2,64,4,64]{1,3,2,0:T(8,128)}, f32[2,64,4,64]{1,3,2,0:T(8,128)}, u32[]{:S(2)}, u32[]{:S(2)}) collective-permute-start(f32[2,64,4,64]{1,3,2,0:T(8,128)} %convolution_bitcast_fusion.4), channel_id=1, source_target_pairs={{0,232},{4,236},{8,240},{12,244},{16,248},{20,252},{24,0},{28,4},{... | collective-permute-start | bytes 393224 | tf_op jit(solution)/shard_map/ppermute | solution.py:13
  241.2 1.8 copy.185
  246.0 1.8 copy.190
  250.8 1.8 copy.195
  255.6 1.8 copy.200
  265.7 4.7 %collective-permute-start.2 = (f32[8,64,4,64]{1,3,2,0:T(8,128)S(1)}, f32[8,64,4,64]{1,3,2,0:T(8,128)S(1)}, u32[]{:S(2)}, u32[]{:S(2)}) collective-permute-start(f32[8,64,4,64]{1,3,2,0:T(8,128)S(1)} %convolution_bitcast_fusion), channel_id=1, source_target_pairs={{0,252},{4,0},{8,4},{12,8},{16,12},{20,16},{24,20},{28,24},{32,28}... | collective-permute-start | bytes 1572872 | tf_op jit(solution)/shard_map/ppermute | solution.py:13
  275.7 7.0 %collective-permute-done.2 = f32[8,64,4,64]{1,3,2,0:T(8,128)S(1)} collective-permute-done((f32[8,64,4,64]{1,3,2,0:T(8,128)S(1)}, f32[8,64,4,64]{1,3,2,0:T(8,128)S(1)}, u32[]{:S(2)}, u32[]{:S(2)}) %collective-permute-start.2) | collective-permute-done | bytes 524320 | tf_op jit(solution)/shard_map/ppermute | solution.py:13
  290.5 5.6 %multiply_reduce_fusion = f32[8,64,4,64]{1,3,2,0:T(8,128)S(1)} fusion(f32[9,8,64,4,64]{2,4,3,1,0:T(8,128)} %bitcast_dynamic-update-slice_fusion, f32[9,8,64,4]{2,3,1,0:T(4,128)S(1)} %get-tuple-element.21), kind=kLoop, calls=%fused_computation.31 | loop fusion | flops 2228224 | bytes 5316608 | tf_op jit(solution)/shard_map/reduce_sum | solution.py:29
  297.6 3.0 fusion.186
  300.6 66.8 %all-reduce.3.cloned.1.call-done = f32[512,1024]{1,0:T(8,128)} async-done(((f32[512,1024]{1,0:T(8,128)}), f32[512,1024]{1,0:T(8,128)}) %all-reduce.3.cloned.1.call-update) | async-done | bytes 2097168 | tf_op jit(solution)/shard_map/psum | solution.py:160
  367.4 2.2 fusion.77
  371.1 9.2 %convolution_convert_fusion = bf16[512,1024]{1,0:T(8,128)(2,1)} fusion(bf16[1024,1024]{1,0:T(8,128)(2,1)S(1)} %copy-done, bf16[512,1024]{1,0:T(8,128)(2,1)} %multiply_convert_fusion, bf16[1024,1024]{1,0:T(8,128)(2,1)} %param.16), kind=kOutput, calls=%fused_computation.54 | convolution fusion | flops 2182086656 | bytes 6291456 | tf_op jit(solution)/shard_map/dot_general | solution.py:169
  384.2 22.1 %reduce-scatter.2.cloned.1.call-done = bf16[512,256]{1,0:T(8,128)(2,1)} async-done(((bf16[512,1024]{1,0:T(8,128)(2,1)}), bf16[512,256]{1,0:T(8,128)(2,1)}) %reduce-scatter.2.cloned.1.call-update) | async-done | bytes 262160 | tf_op jit(solution)/shard_map/reduce_scatter | solution.py:168
  407.5 8.5 %all-reduce = (f32[512]{0:T(512)S(1)}, f32[512]{0:T(512)S(1)}) all-reduce(f32[512]{0:T(512)S(1)} %get-tuple-element.17, f32[512]{0:T(512)S(1)} %get-tuple-element.16), channel_id=1, replica_groups=mesh['req'=64,'tp'=4] {'tp'}, use_global_device_ids=true, to_apply=%region_46.47 | all-reduce | flops 1024 | bytes 8192 | tf_op jit(solution)/shard_map/psum | solution.py:175
  416.0 1.9 multiply_convert_fusion.1
  (354 shorter events, 131.2 us)
Async XLA Ops:
  7.2 363.9 %copy-start = (bf16[1024,1024]{1,0:T(8,128)(2,1)S(1)}, bf16[1024,1024]{1,0:T(8,128)(2,1)}, u32[]{:S(2)}) copy-start(bf16[1024,1024]{1,0:T(8,128)(2,1)} %param.17) | copy-start | bytes 6291460
  7.2 137.3 %all-gather.2.cloned.1.call-start = ((), (), s32[]{:S(2)}) async-start(), calls=%async_computation.1 | async-start | bytes 1310720 | tf_op jit(solution)/shard_map/all_gather | solution.py:102
  9.0 42.3 %collective-permute-start.7 = (bf16[2]{0:T(256)(128)(2,1)S(1)}, bf16[2]{0:T(256)(128)(2,1)S(1)}, u32[]{:S(2)}, u32[]{:S(2)}) collective-permute-start(bf16[2]{0:T(256)(128)(2,1)S(1)} %get-tuple-element.60), channel_id=1, source_target_pairs={{0,12},{4,16},{8,20},{12,24},{16,28},{20,32},{24,36},{28,40},{32,4... | collective-permute-start | bytes 20 | tf_op jit(solution)/shard_map/ppermute | solution.py:13
  9.9 44.3 %collective-permute-start.3 = (bf16[2]{0:T(256)(128)(2,1)S(1)}, bf16[2]{0:T(256)(128)(2,1)S(1)}, u32[]{:S(2)}, u32[]{:S(2)}) collective-permute-start(bf16[2]{0:T(256)(128)(2,1)S(1)} %get-tuple-element.60), channel_id=1, source_target_pairs={{0,8},{4,12},{8,16},{12,20},{16,24},{20,28},{24,32},{28,36},{32,40... | collective-permute-start | bytes 20 | tf_op jit(solution)/shard_map/ppermute | solution.py:13
  11.1 62.6 %collective-permute-start.15 = (bf16[2]{0:T(256)(128)(2,1)S(1)}, bf16[2]{0:T(256)(128)(2,1)S(1)}, u32[]{:S(2)}, u32[]{:S(2)}) collective-permute-start(bf16[2]{0:T(256)(128)(2,1)S(1)} %get-tuple-element.60), channel_id=1, source_target_pairs={{0,20},{4,24},{8,28},{12,32},{16,36},{20,40},{24,44},{28,48},{32,5... | collective-permute-start | bytes 20 | tf_op jit(solution)/shard_map/ppermute | solution.py:13
  15.4 60.7 %collective-permute-start.11 = (bf16[2]{0:T(256)(128)(2,1)S(1)}, bf16[2]{0:T(256)(128)(2,1)S(1)}, u32[]{:S(2)}, u32[]{:S(2)}) collective-permute-start(bf16[2]{0:T(256)(128)(2,1)S(1)} %get-tuple-element.60), channel_id=1, source_target_pairs={{0,16},{4,20},{8,24},{12,28},{16,32},{20,36},{24,40},{28,44},{32,4... | collective-permute-start | bytes 20 | tf_op jit(solution)/shard_map/ppermute | solution.py:13
  16.7 81.7 %collective-permute-start.23 = (bf16[2]{0:T(256)(128)(2,1)S(1)}, bf16[2]{0:T(256)(128)(2,1)S(1)}, u32[]{:S(2)}, u32[]{:S(2)}) collective-permute-start(bf16[2]{0:T(256)(128)(2,1)S(1)} %get-tuple-element.60), channel_id=1, source_target_pairs={{0,28},{4,32},{8,36},{12,40},{16,44},{20,48},{24,52},{28,56},{32,6... | collective-permute-start | bytes 20 | tf_op jit(solution)/shard_map/ppermute | solution.py:13
  17.4 350.0 %all-reduce.3.cloned.1.call-start = ((), (), s32[]{:S(2)}) async-start(), calls=%async_computation.2 | async-start | bytes 4194304 | tf_op jit(solution)/shard_map/psum | solution.py:160
  51.3 49.1 %collective-permute-start.19 = (bf16[2]{0:T(256)(128)(2,1)S(1)}, bf16[2]{0:T(256)(128)(2,1)S(1)}, u32[]{:S(2)}, u32[]{:S(2)}) collective-permute-start(bf16[2]{0:T(256)(128)(2,1)S(1)} %get-tuple-element.60), channel_id=1, source_target_pairs={{0,24},{4,28},{8,32},{12,36},{16,40},{20,44},{24,48},{28,52},{32,5... | collective-permute-start | bytes 20 | tf_op jit(solution)/shard_map/ppermute | solution.py:13
  54.2 90.3 %collective-permute-start = (bf16[8,128]{1,0:T(8,128)(2,1)S(1)}, bf16[8,128]{1,0:T(8,128)(2,1)S(1)}, u32[]{:S(2)}, u32[]{:S(2)}) collective-permute-start(bf16[8,128]{1,0:T(8,128)(2,1)S(1)} %get-tuple-element.53), channel_id=1, source_target_pairs={{0,4},{4,8},{8,12},{12,16},{16,20},{20,24},{24,28},{28,32},{32,36}... | collective-permute-start | bytes 6152 | tf_op jit(solution)/shard_map/ppermute | solution.py:13
  73.7 65.1 %collective-permute-start.4 = (bf16[2,128]{1,0:T(2,128)(2,1)S(1)}, bf16[2,128]{1,0:T(2,128)(2,1)S(1)}, u32[]{:S(2)}, u32[]{:S(2)}) collective-permute-start(bf16[2,128]{1,0:T(2,128)(2,1)S(1)} %convert_element_type.237), channel_id=1, source_target_pairs={{0,8},{4,12},{8,16},{12,20},{16,24},{20,28},{24,32},{28,36},{32,40... | collective-permute-start | bytes 1544 | tf_op jit(solution)/shard_map/ppermute | solution.py:13
  76.1 62.7 %collective-permute-start.8 = (bf16[2,128]{1,0:T(2,128)(2,1)S(1)}, bf16[2,128]{1,0:T(2,128)(2,1)S(1)}, u32[]{:S(2)}, u32[]{:S(2)}) collective-permute-start(bf16[2,128]{1,0:T(2,128)(2,1)S(1)} %convert_element_type.241), channel_id=1, source_target_pairs={{0,12},{4,16},{8,20},{12,24},{16,28},{20,32},{24,36},{28,40},{32,4... | collective-permute-start | bytes 1544 | tf_op jit(solution)/shard_map/ppermute | solution.py:13
  98.3 42.3 %collective-permute-start.12 = (bf16[2,128]{1,0:T(2,128)(2,1)S(1)}, bf16[2,128]{1,0:T(2,128)(2,1)S(1)}, u32[]{:S(2)}, u32[]{:S(2)}) collective-permute-start(bf16[2,128]{1,0:T(2,128)(2,1)S(1)} %convert_element_type.245), channel_id=1, source_target_pairs={{0,16},{4,20},{8,24},{12,28},{16,32},{20,36},{24,40},{28,44},{32,4... | collective-permute-start | bytes 1544 | tf_op jit(solution)/shard_map/ppermute | solution.py:13
  100.4 40.3 %collective-permute-start.16 = (bf16[2,128]{1,0:T(2,128)(2,1)S(1)}, bf16[2,128]{1,0:T(2,128)(2,1)S(1)}, u32[]{:S(2)}, u32[]{:S(2)}) collective-permute-start(bf16[2,128]{1,0:T(2,128)(2,1)S(1)} %convert_element_type.249), channel_id=1, source_target_pairs={{0,20},{4,24},{8,28},{12,32},{16,36},{20,40},{24,44},{28,48},{32,5... | collective-permute-start | bytes 1544 | tf_op jit(solution)/shard_map/ppermute | solution.py:13
  138.8 5.7 %collective-permute-start.20 = (bf16[2,128]{1,0:T(2,128)(2,1)S(1)}, bf16[2,128]{1,0:T(2,128)(2,1)S(1)}, u32[]{:S(2)}, u32[]{:S(2)}) collective-permute-start(bf16[2,128]{1,0:T(2,128)(2,1)S(1)} %convert_element_type.253), channel_id=1, source_target_pairs={{0,24},{4,28},{8,32},{12,36},{16,40},{20,44},{24,48},{28,52},{32,5... | collective-permute-start | bytes 1544 | tf_op jit(solution)/shard_map/ppermute | solution.py:13
  138.8 5.6 %collective-permute-start.24 = (bf16[2,128]{1,0:T(2,128)(2,1)S(1)}, bf16[2,128]{1,0:T(2,128)(2,1)S(1)}, u32[]{:S(2)}, u32[]{:S(2)}) collective-permute-start(bf16[2,128]{1,0:T(2,128)(2,1)S(1)} %convert_element_type.257), channel_id=1, source_target_pairs={{0,28},{4,32},{8,36},{12,40},{16,44},{20,48},{24,52},{28,56},{32,6... | collective-permute-start | bytes 1544 | tf_op jit(solution)/shard_map/ppermute | solution.py:13
  153.2 17.6 %collective-permute-start.5 = (bf16[2,64,4,64]{3,1,2,0:T(8,128)(2,1)}, bf16[2,64,4,64]{3,1,2,0:T(8,128)(2,1)}, u32[]{:S(2)}, u32[]{:S(2)}) collective-permute-start(bf16[2,64,4,64]{3,1,2,0:T(8,128)(2,1)} %gather_fusion.2), channel_id=1, source_target_pairs={{0,8},{4,12},{8,16},{12,20},{16,24},{20,28},{24,32},{28,36},{32,40... | collective-permute-start | bytes 196616 | tf_op jit(solution)/shard_map/ppermute | solution.py:13
  154.7 18.2 %collective-permute-start.9 = (bf16[2,64,4,64]{3,1,2,0:T(8,128)(2,1)}, bf16[2,64,4,64]{3,1,2,0:T(8,128)(2,1)}, u32[]{:S(2)}, u32[]{:S(2)}) collective-permute-start(bf16[2,64,4,64]{3,1,2,0:T(8,128)(2,1)} %gather_fusion.2), channel_id=1, source_target_pairs={{0,12},{4,16},{8,20},{12,24},{16,28},{20,32},{24,36},{28,40},{32,4... | collective-permute-start | bytes 196616 | tf_op jit(solution)/shard_map/ppermute | solution.py:13
  154.7 22.1 %collective-permute-start.13 = (bf16[2,64,4,64]{3,1,2,0:T(8,128)(2,1)}, bf16[2,64,4,64]{3,1,2,0:T(8,128)(2,1)}, u32[]{:S(2)}, u32[]{:S(2)}) collective-permute-start(bf16[2,64,4,64]{3,1,2,0:T(8,128)(2,1)} %gather_fusion.2), channel_id=1, source_target_pairs={{0,16},{4,20},{8,24},{12,28},{16,32},{20,36},{24,40},{28,44},{32,4... | collective-permute-start | bytes 196616 | tf_op jit(solution)/shard_map/ppermute | solution.py:13
  156.9 25.3 %collective-permute-start.17 = (bf16[2,64,4,64]{3,1,2,0:T(8,128)(2,1)}, bf16[2,64,4,64]{3,1,2,0:T(8,128)(2,1)}, u32[]{:S(2)}, u32[]{:S(2)}) collective-permute-start(bf16[2,64,4,64]{3,1,2,0:T(8,128)(2,1)} %gather_fusion.2), channel_id=1, source_target_pairs={{0,20},{4,24},{8,28},{12,32},{16,36},{20,40},{24,44},{28,48},{32,5... | collective-permute-start | bytes 196616 | tf_op jit(solution)/shard_map/ppermute | solution.py:13
  158.4 29.3 %collective-permute-start.21 = (bf16[2,64,4,64]{3,1,2,0:T(8,128)(2,1)}, bf16[2,64,4,64]{3,1,2,0:T(8,128)(2,1)}, u32[]{:S(2)}, u32[]{:S(2)}) collective-permute-start(bf16[2,64,4,64]{3,1,2,0:T(8,128)(2,1)} %gather_fusion.2), channel_id=1, source_target_pairs={{0,24},{4,28},{8,32},{12,36},{16,40},{20,44},{24,48},{28,52},{32,5... | collective-permute-start | bytes 196616 | tf_op jit(solution)/shard_map/ppermute | solution.py:13
  170.9 18.4 %collective-permute-start.25 = (bf16[2,64,4,64]{3,1,2,0:T(8,128)(2,1)S(1)}, bf16[2,64,4,64]{3,1,2,0:T(8,128)(2,1)S(1)}, u32[]{:S(2)}, u32[]{:S(2)}) collective-permute-start(bf16[2,64,4,64]{3,1,2,0:T(8,128)(2,1)S(1)} %copy-done.31), channel_id=1, source_target_pairs={{0,28},{4,32},{8,36},{12,40},{16,44},{20,48},{24,52},{28,56},{32,6... | collective-permute-start | bytes 196616 | tf_op jit(solution)/shard_map/ppermute | solution.py:13
  172.9 20.0 %collective-permute-start.35 = (f32[2,4,64]{2,1,0:T(4,128)S(1)}, f32[2,4,64]{2,1,0:T(4,128)S(1)}, u32[]{:S(2)}, u32[]{:S(2)}) collective-permute-start(f32[2,4,64]{2,1,0:T(4,128)S(1)} %convert_reduce_fusion.8), channel_id=1, source_target_pairs={{0,248},{4,252},{8,0},{12,4},{16,8},{20,12},{24,16},{28,20},{32,24... | collective-permute-start | bytes 6152 | tf_op jit(solution)/shard_map/ppermute | solution.py:13
  176.8 16.7 %collective-permute-start.36 = (f32[2,4,64]{2,1,0:T(4,128)S(1)}, f32[2,4,64]{2,1,0:T(4,128)S(1)}, u32[]{:S(2)}, u32[]{:S(2)}) collective-permute-start(f32[2,4,64]{2,1,0:T(4,128)S(1)} %convert_reduce_fusion.7), channel_id=1, source_target_pairs={{0,244},{4,248},{8,252},{12,0},{16,4},{20,8},{24,12},{28,16},{32,2... | collective-permute-start | bytes 6152 | tf_op jit(solution)/shard_map/ppermute | solution.py:13
  181.9 27.9 %copy-start.19 = (bf16[2,128,1,256]{1,3,0,2:T(8,128)(2,1)S(1)}, bf16[2,128,1,256]{1,3,0,2:T(8,128)(2,1)}, u32[]{:S(2)}) copy-start(bf16[2,128,1,256]{1,3,0,2:T(8,128)(2,1)} %copy.198) | copy-start | bytes 393220
  182.2 15.5 %collective-permute-start.37 = (f32[2,4,64]{2,1,0:T(4,128)S(1)}, f32[2,4,64]{2,1,0:T(4,128)S(1)}, u32[]{:S(2)}, u32[]{:S(2)}) collective-permute-start(f32[2,4,64]{2,1,0:T(4,128)S(1)} %convert_reduce_fusion.6), channel_id=1, source_target_pairs={{0,240},{4,244},{8,248},{12,252},{16,0},{20,4},{24,8},{28,12},{32,... | collective-permute-start | bytes 6152 | tf_op jit(solution)/shard_map/ppermute | solution.py:13
  187.7 10.7 %collective-permute-start.38 = (f32[2,4,64]{2,1,0:T(4,128)S(1)}, f32[2,4,64]{2,1,0:T(4,128)S(1)}, u32[]{:S(2)}, u32[]{:S(2)}) collective-permute-start(f32[2,4,64]{2,1,0:T(4,128)S(1)} %convert_reduce_fusion.5), channel_id=1, source_target_pairs={{0,236},{4,240},{8,244},{12,248},{16,252},{20,0},{24,4},{28,8},{32... | collective-permute-start | bytes 6152 | tf_op jit(solution)/shard_map/ppermute | solution.py:13
  189.3 9.1 %collective-permute-start.39 = (f32[2,4,64]{2,1,0:T(4,128)S(1)}, f32[2,4,64]{2,1,0:T(4,128)S(1)}, u32[]{:S(2)}, u32[]{:S(2)}) collective-permute-start(f32[2,4,64]{2,1,0:T(4,128)S(1)} %convert_reduce_fusion.4), channel_id=1, source_target_pairs={{0,232},{4,236},{8,240},{12,244},{16,248},{20,252},{24,0},{28,4},{... | collective-permute-start | bytes 6152 | tf_op jit(solution)/shard_map/ppermute | solution.py:13
  192.9 11.3 %collective-permute-start.28 = (f32[2,4,64]{2,1,0:T(4,128)S(1)}, f32[2,4,64]{2,1,0:T(4,128)S(1)}, u32[]{:S(2)}, u32[]{:S(2)}) collective-permute-start(f32[2,4,64]{2,1,0:T(4,128)S(1)} %get-tuple-element.70), channel_id=1, source_target_pairs={{0,248},{4,252},{8,0},{12,4},{16,8},{20,12},{24,16},{28,20},{32,24... | collective-permute-start | bytes 6152 | tf_op jit(solution)/shard_map/ppermute | solution.py:13
  193.5 13.7 %collective-permute-start.29 = (f32[2,4,64]{2,1,0:T(4,128)S(1)}, f32[2,4,64]{2,1,0:T(4,128)S(1)}, u32[]{:S(2)}, u32[]{:S(2)}) collective-permute-start(f32[2,4,64]{2,1,0:T(4,128)S(1)} %get-tuple-element.72), channel_id=1, source_target_pairs={{0,244},{4,248},{8,252},{12,0},{16,4},{20,8},{24,12},{28,16},{32,2... | collective-permute-start | bytes 6152 | tf_op jit(solution)/shard_map/ppermute | solution.py:13
  197.7 9.6 %collective-permute-start.30 = (f32[2,4,64]{2,1,0:T(4,128)S(1)}, f32[2,4,64]{2,1,0:T(4,128)S(1)}, u32[]{:S(2)}, u32[]{:S(2)}) collective-permute-start(f32[2,4,64]{2,1,0:T(4,128)S(1)} %get-tuple-element.74), channel_id=1, source_target_pairs={{0,240},{4,244},{8,248},{12,252},{16,0},{20,4},{24,8},{28,12},{32,... | collective-permute-start | bytes 6152 | tf_op jit(solution)/shard_map/ppermute | solution.py:13
  198.5 10.2 %collective-permute-start.31 = (f32[2,4,64]{2,1,0:T(4,128)S(1)}, f32[2,4,64]{2,1,0:T(4,128)S(1)}, u32[]{:S(2)}, u32[]{:S(2)}) collective-permute-start(f32[2,4,64]{2,1,0:T(4,128)S(1)} %get-tuple-element.76), channel_id=1, source_target_pairs={{0,236},{4,240},{8,244},{12,248},{16,252},{20,0},{24,4},{28,8},{32... | collective-permute-start | bytes 6152 | tf_op jit(solution)/shard_map/ppermute | solution.py:13
  198.5 5.7 %collective-permute-start.40 = (f32[2,4,64]{2,1,0:T(4,128)S(1)}, f32[2,4,64]{2,1,0:T(4,128)S(1)}, u32[]{:S(2)}, u32[]{:S(2)}) collective-permute-start(f32[2,4,64]{2,1,0:T(4,128)S(1)} %convert_reduce_fusion.3), channel_id=1, source_target_pairs={{0,228},{4,232},{8,236},{12,240},{16,244},{20,248},{24,252},{28,0}... | collective-permute-start | bytes 6152 | tf_op jit(solution)/shard_map/ppermute | solution.py:13
  204.2 56.2 %collective-permute-start.1 = (bf16[8,64,4,64]{3,1,2,0:T(8,128)(2,1)}, bf16[8,64,4,64]{3,1,2,0:T(8,128)(2,1)}, u32[]{:S(2)}, u32[]{:S(2)}) collective-permute-start(bf16[8,64,4,64]{3,1,2,0:T(8,128)(2,1)} %copy.159), channel_id=1, source_target_pairs={{0,4},{4,8},{8,12},{12,16},{16,20},{20,24},{24,28},{28,32},{32,36}... | collective-permute-start | bytes 786440 | tf_op jit(solution)/shard_map/ppermute | solution.py:13
  204.2 6.7 %collective-permute-start.32 = (f32[2,4,64]{2,1,0:T(4,128)S(1)}, f32[2,4,64]{2,1,0:T(4,128)S(1)}, u32[]{:S(2)}, u32[]{:S(2)}) collective-permute-start(f32[2,4,64]{2,1,0:T(4,128)S(1)} %get-tuple-element.78), channel_id=1, source_target_pairs={{0,232},{4,236},{8,240},{12,244},{16,248},{20,252},{24,0},{28,4},{... | collective-permute-start | bytes 6152 | tf_op jit(solution)/shard_map/ppermute | solution.py:13
  207.3 5.9 %collective-permute-start.33 = (f32[2,4,64]{2,1,0:T(4,128)S(1)}, f32[2,4,64]{2,1,0:T(4,128)S(1)}, u32[]{:S(2)}, u32[]{:S(2)}) collective-permute-start(f32[2,4,64]{2,1,0:T(4,128)S(1)} %get-tuple-element.80), channel_id=1, source_target_pairs={{0,228},{4,232},{8,236},{12,240},{16,244},{20,248},{24,252},{28,0}... | collective-permute-start | bytes 6152 | tf_op jit(solution)/shard_map/ppermute | solution.py:13
  207.3 11.0 %collective-permute-start.6 = (f32[2,64,4,64]{1,3,2,0:T(8,128)S(1)}, f32[2,64,4,64]{1,3,2,0:T(8,128)S(1)}, u32[]{:S(2)}, u32[]{:S(2)}) collective-permute-start(f32[2,64,4,64]{1,3,2,0:T(8,128)S(1)} %convolution_bitcast_fusion.8), channel_id=1, source_target_pairs={{0,248},{4,252},{8,0},{12,4},{16,8},{20,12},{24,16},{28,20},{32,24... | collective-permute-start | bytes 393224 | tf_op jit(solution)/shard_map/ppermute | solution.py:13
  208.6 14.4 %collective-permute-start.10 = (f32[2,64,4,64]{1,3,2,0:T(8,128)S(1)}, f32[2,64,4,64]{1,3,2,0:T(8,128)S(1)}, u32[]{:S(2)}, u32[]{:S(2)}) collective-permute-start(f32[2,64,4,64]{1,3,2,0:T(8,128)S(1)} %convolution_bitcast_fusion.7), channel_id=1, source_target_pairs={{0,244},{4,248},{8,252},{12,0},{16,4},{20,8},{24,12},{28,16},{32,2... | collective-permute-start | bytes 393224 | tf_op jit(solution)/shard_map/ppermute | solution.py:13
  210.9 30.3 %collective-permute-start.14 = (f32[2,64,4,64]{1,3,2,0:T(8,128)}, f32[2,64,4,64]{1,3,2,0:T(8,128)}, u32[]{:S(2)}, u32[]{:S(2)}) collective-permute-start(f32[2,64,4,64]{1,3,2,0:T(8,128)} %convolution_bitcast_fusion.6), channel_id=1, source_target_pairs={{0,240},{4,244},{8,248},{12,252},{16,0},{20,4},{24,8},{28,12},{32,... | collective-permute-start | bytes 393224 | tf_op jit(solution)/shard_map/ppermute | solution.py:13
  213.1 32.8 %collective-permute-start.18 = (f32[2,64,4,64]{1,3,2,0:T(8,128)}, f32[2,64,4,64]{1,3,2,0:T(8,128)}, u32[]{:S(2)}, u32[]{:S(2)}) collective-permute-start(f32[2,64,4,64]{1,3,2,0:T(8,128)} %convolution_bitcast_fusion.5), channel_id=1, source_target_pairs={{0,236},{4,240},{8,244},{12,248},{16,252},{20,0},{24,4},{28,8},{32... | collective-permute-start | bytes 393224 | tf_op jit(solution)/shard_map/ppermute | solution.py:13
  218.3 32.5 %collective-permute-start.22 = (f32[2,64,4,64]{1,3,2,0:T(8,128)}, f32[2,64,4,64]{1,3,2,0:T(8,128)}, u32[]{:S(2)}, u32[]{:S(2)}) collective-permute-start(f32[2,64,4,64]{1,3,2,0:T(8,128)} %convolution_bitcast_fusion.4), channel_id=1, source_target_pairs={{0,232},{4,236},{8,240},{12,244},{16,248},{20,252},{24,0},{28,4},{... | collective-permute-start | bytes 393224 | tf_op jit(solution)/shard_map/ppermute | solution.py:13
  223.8 31.8 %collective-permute-start.26 = (f32[2,64,4,64]{1,3,2,0:T(8,128)}, f32[2,64,4,64]{1,3,2,0:T(8,128)}, u32[]{:S(2)}, u32[]{:S(2)}) collective-permute-start(f32[2,64,4,64]{1,3,2,0:T(8,128)} %convolution_bitcast_fusion.3), channel_id=1, source_target_pairs={{0,228},{4,232},{8,236},{12,240},{16,244},{20,248},{24,252},{28,0}... | collective-permute-start | bytes 393224 | tf_op jit(solution)/shard_map/ppermute | solution.py:13
  262.2 12.4 %collective-permute-start.27 = (f32[8,4,64]{2,1,0:T(4,128)S(1)}, f32[8,4,64]{2,1,0:T(4,128)S(1)}, u32[]{:S(2)}, u32[]{:S(2)}) collective-permute-start(f32[8,4,64]{2,1,0:T(4,128)S(1)} %get-tuple-element.68), channel_id=1, source_target_pairs={{0,252},{4,0},{8,4},{12,8},{16,12},{20,16},{24,20},{28,24},{32,28}... | collective-permute-start | bytes 24584 | tf_op jit(solution)/shard_map/ppermute | solution.py:13
  264.0 6.4 %collective-permute-start.34 = (f32[8,4,64]{2,1,0:T(4,128)S(1)}, f32[8,4,64]{2,1,0:T(4,128)S(1)}, u32[]{:S(2)}, u32[]{:S(2)}) collective-permute-start(f32[8,4,64]{2,1,0:T(4,128)S(1)} %convert_reduce_fusion), channel_id=1, source_target_pairs={{0,252},{4,0},{8,4},{12,8},{16,12},{20,16},{24,20},{28,24},{32,28}... | collective-permute-start | bytes 24584 | tf_op jit(solution)/shard_map/ppermute | solution.py:13
  265.7 17.0 %collective-permute-start.2 = (f32[8,64,4,64]{1,3,2,0:T(8,128)S(1)}, f32[8,64,4,64]{1,3,2,0:T(8,128)S(1)}, u32[]{:S(2)}, u32[]{:S(2)}) collective-permute-start(f32[8,64,4,64]{1,3,2,0:T(8,128)S(1)} %convolution_bitcast_fusion), channel_id=1, source_target_pairs={{0,252},{4,0},{8,4},{12,8},{16,12},{20,16},{24,20},{28,24},{32,28}... | collective-permute-start | bytes 1572872 | tf_op jit(solution)/shard_map/ppermute | solution.py:13
  297.6 69.8 %copy-start.8 = (bf16[512,1024]{1,0:T(8,128)(2,1)S(1)}, bf16[512,1024]{1,0:T(8,128)(2,1)}, u32[]{:S(2)}) copy-start(bf16[512,1024]{1,0:T(8,128)(2,1)} %all-gather.2.cloned.1.call-done) | copy-start | bytes 3145732
  300.6 69.0 %copy-start.45 = (f32[1024]{0:T(1024)S(1)}, f32[1024]{0:T(1024)}, u32[]{:S(2)}) copy-start(f32[1024]{0:T(1024)} %param.15) | copy-start | bytes 12292
  300.6 105.7 %reduce-scatter.2.cloned.1.call-start = ((), (), s32[]{:S(2)}) async-start(), calls=%async_computation.3 | async-start | bytes 1310720 | tf_op jit(solution)/shard_map/reduce_scatter | solution.py:168
  (44 other events, 358.4 us)
Sparse Core Ops, SparseCore 0:
  17.5 30.9 all-gather.1
  300.7 66.6 all-reduce.2
  380.4 25.8 reduce-scatter.1
where the time goes:
time: 430 us; the launch traced here: 425 us
  waiting for transfers between devices  105 us (24%)
  local copies, waits for them, and re-layouts  102 us (24%)
  matrix products  102 us (24%)
  starting transfers between devices  72.5 us (17%)
  other arithmetic  19.6 us (5%)
  between operations  15.3 us (4%)
  blocking collectives  8.47 us (2%)
    ppermute x41, starting transfers between devices, from_behind(): lax.ppermute(value, axis, [(i, (i + by) % size) for i in range(size)])  72.2 us
    psum x1, waiting for transfers between devices, shards(): summed = lax.psum(branch, 'tp')  66.8 us
    dot_general x8, matrix products, page_rows(): jnp.einsum('rs,spcf->rpcf', picker, cache_pool, preferred_element_type=jn...  64.3 us
    reduce_scatter x1, waiting for transfers between devices, shards(): lax.psum_scatter(jnp.dot(inner, w_down, preferred_element_type=jnp.float3...  22.1 us
    slice x16, local copies, waits for them, and re-layouts, rows_split(): rows[:, :, 0].reshape(requests, page_len, heads_local, HD)  19.2 us
    scatter x12, local copies, waits for them, and re-layouts, spread_back(): jnp.zeros((requests,) + arrived[0].shape[1:], jnp.float32).at[long_ids]  17.2 us
    ppermute x41, waiting for transfers between devices, from_behind(): lax.ppermute(value, axis, [(i, (i + by) % size) for i in range(size)])  16.4 us
    unnamed x119, local copies, waits for them, and re-layouts  14.9 us
  transfers between devices with their start and end apart: 44, of which 6 were waited for; matrix products, arithmetic and copies ran while one was open for 42% of the time, Pallas kernels for 0%

commit v1 on v0

--- a/solution.py
+++ b/solution.py
@@ -157,7 +157,8 @@
     )
     branch = jnp.dot(attended, w_out, preferred_element_type=jnp.float32)
     second_share = lax.dynamic_slice_in_dim(second_gain, start, share, 0)
-    summed = lax.psum(branch, "tp")
+    w2 = jax.lax.all_gather(branch, axis_name="tp")
+    summed = jnp.sum(w2, 0)
     mixed_all = gathered.astype(jnp.float32) + summed
     whole_sums = (jnp.sum(mixed_all, axis=-1), jnp.sum(mixed_all * mixed_all, axis=-1))
     normed_all = norm_from_sums(mixed_all, whole_sums, first_gain, width_all).astype(jnp.bfloat16)

time: 430 us -> 458 us (1.065)
  waiting for transfers between devices: 105 us -> 128 us
  other arithmetic: 19.6 us -> 25.6 us
    all_gather x0 -> x1, waiting for transfers between devices: none -> 88.6 us  [shards(): w2 = jax.lax.all_gather(branch, axis_name='tp')]
    psum x1 -> x0, waiting for transfers between devices: 66.8 us -> none  [shards(): summed = lax.psum(branch, 'tp')]
    reduce_sum x0 -> x1, other arithmetic: none -> 5.99 us  [shards(): summed = jnp.sum(w2, 0)]
  transfers between devices with their start and end apart: 44 -> 44, of which waited for: 6 -> 6; matrix products, arithmetic and copies ran while one was open for 42% -> 39% of each run, Pallas kernels for 0% -> 0%
where the time goes in v1:
time: 458 us; the launch traced here: 453 us
  waiting for transfers between devices  128 us (28%)
  matrix products  102 us (22%)
  local copies, waits for them, and re-layouts  101 us (22%)
  starting transfers between devices  72.5 us (16%)
  other arithmetic  25.6 us (6%)
  between operations  15.3 us (3%)
  blocking collectives  8.47 us (2%)
    all_gather x1, waiting for transfers between devices, shards(): w2 = jax.lax.all_gather(branch, axis_name='tp')  88.6 us
    ppermute x41, starting transfers between devices, from_behind(): lax.ppermute(value, axis, [(i, (i + by) % size) for i in range(size)])  72.2 us
    dot_general x8, matrix products, page_rows(): jnp.einsum('rs,spcf->rpcf', picker, cache_pool, preferred_element_type=jn...  64.3 us
    reduce_scatter x1, waiting for transfers between devices, shards(): lax.psum_scatter(jnp.dot(inner, w_down, preferred_element_type=jnp.float3...  23.2 us
    slice x16, local copies, waits for them, and re-layouts, rows_split(): rows[:, :, 0].reshape(requests, page_len, heads_local, HD)  19.1 us
    scatter x12, local copies, waits for them, and re-layouts, spread_back(): jnp.zeros((requests,) + arrived[0].shape[1:], jnp.float32).at[long_ids]  17.2 us
    ppermute x41, waiting for transfers between devices, from_behind(): lax.ppermute(value, axis, [(i, (i + by) % size) for i in range(size)])  16.4 us
    unnamed x119, local copies, waits for them, and re-layouts  14.9 us
  transfers between devices with their start and end apart: 44, of which 6 were waited for; matrix products, arithmetic and copies ran while one was open for 39% of the time, Pallas kernels for 0%

profile of v1, /device:TPU:2, one launch (start us, length us, event | category | flops | bytes accessed | tf_op | source)
XLA Modules:
  0.0 452.9 jit_solution(8334085113621228535)
XLA Ops:
  11.1 4.3 collective-permute-start.15
  21.2 7.9 %convolution_convert_fusion.2 = bf16[8,128,2,256]{3,0,2,1:T(8,128)(2,1)S(1)} fusion(bf16[64,128,2,256]{3,2,1,0:T(2,128)(2,1)} %param.19, s32[8]{0:T(128)S(1)} %get-tuple-element.46), kind=kOutput, calls=%fused_computation.56 | convolution fusion | flops 67633664 | bytes 9437216 | tf_op jit(solution)/shard_map/rs,spcf->rpcf/dot_general | solution.py:46
  31.6 2.3 copy.165
  33.9 8.4 %convolution_convert_fusion.1 = bf16[8,128,2,256]{3,0,2,1:T(8,128)(2,1)S(1)} fusion(bf16[64,128,2,256]{3,2,1,0:T(2,128)(2,1)} %param.19, s32[8]{0:T(128)S(1)} %get-tuple-element.45), kind=kOutput, calls=%fused_computation.55 | convolution fusion | flops 67633664 | bytes 9437216 | tf_op jit(solution)/shard_map/rs,spcf->rpcf/dot_general | solution.py:46
  43.3 2.2 copy.168
  45.5 2.2 copy.170
  51.3 2.9 collective-permute-start.19
  55.3 8.0 %fusion.26 = bf16[2,128,2,256]{3,0,2,1:T(2,128)(2,1)S(1)} fusion(bf16[64,128,2,256]{3,2,1,0:T(2,128)(2,1)} %param.19, s32[2]{0:T(128)S(1)} %gather_fusion), kind=kOutput, calls=%fused_computation.77 | convolution fusion | flops 16908416 | bytes 8650760 | tf_op jit(solution)/shard_map/rs,spcf->rpcf/dot_general | solution.py:46
  64.8 8.0 %fusion.29 = bf16[2,128,2,256]{3,0,2,1:T(2,128)(2,1)S(1)} fusion(bf16[64,128,2,256]{3,2,1,0:T(2,128)(2,1)} %param.19, s32[2]{0:T(128)S(1)} %gather_fusion.3), kind=kOutput, calls=%fused_computation.78 | convolution fusion | flops 16908416 | bytes 8650760 | tf_op jit(solution)/shard_map/rs,spcf->rpcf/dot_general | solution.py:46
  73.6 2.4 collective-permute-start.4
  76.1 3.1 collective-permute-start.8
  79.9 8.0 %fusion.32 = bf16[2,128,2,256]{3,0,2,1:T(2,128)(2,1)S(1)} fusion(bf16[64,128,2,256]{3,2,1,0:T(2,128)(2,1)} %param.19, s32[2]{0:T(128)S(1)} %gather_fusion.5), kind=kOutput, calls=%fused_computation.79 | convolution fusion | flops 16908416 | bytes 8650760 | tf_op jit(solution)/shard_map/rs,spcf->rpcf/dot_general | solution.py:46
  89.4 8.0 %fusion.35 = bf16[2,128,2,256]{3,0,2,1:T(2,128)(2,1)S(1)} fusion(bf16[64,128,2,256]{3,2,1,0:T(2,128)(2,1)} %param.19, s32[2]{0:T(128)S(1)} %gather_fusion.7), kind=kOutput, calls=%fused_computation.80 | convolution fusion | flops 16908416 | bytes 8650760 | tf_op jit(solution)/shard_map/rs,spcf->rpcf/dot_general | solution.py:46
  98.3 2.0 collective-permute-start.12
  100.3 3.7 collective-permute-start.16
  104.7 8.0 %fusion.38 = bf16[2,128,2,256]{3,0,2,1:T(2,128)(2,1)S(1)} fusion(bf16[64,128,2,256]{3,2,1,0:T(2,128)(2,1)} %param.19, s32[2]{0:T(128)S(1)} %gather_fusion.9), kind=kOutput, calls=%fused_computation.81 | convolution fusion | flops 16908416 | bytes 8650760 | tf_op jit(solution)/shard_map/rs,spcf->rpcf/dot_general | solution.py:46
  114.2 8.0 %fusion.41 = bf16[2,128,2,256]{3,0,2,1:T(2,128)(2,1)S(1)} fusion(bf16[64,128,2,256]{3,2,1,0:T(2,128)(2,1)} %param.19, s32[2]{0:T(128)S(1)} %gather_fusion.11), kind=kOutput, calls=%fused_computation.82 | convolution fusion | flops 16908416 | bytes 8650760 | tf_op jit(solution)/shard_map/rs,spcf->rpcf/dot_general | solution.py:46
  138.7 1.8 collective-permute-start.24
  140.6 3.8 collective-permute-done.20
  144.5 2.7 fusion.45
  150.9 2.3 gather_fusion.2
  154.7 2.2 collective-permute-start.13
  159.1 2.0 convert_element_type.221
  161.1 2.0 convert_element_type.227
  172.8 2.1 collective-permute-start.35
  176.7 2.9 collective-permute-start.36
  182.1 3.0 collective-permute-start.37
  189.2 3.0 collective-permute-start.39
  193.5 4.2 collective-permute-start.29
  198.4 4.0 collective-permute-start.40
  204.1 3.1 collective-permute-start.32
  210.8 2.2 collective-permute-start.14
  213.3 4.9 %collective-permute-done.6 = f32[2,64,4,64]{1,3,2,0:T(8,128)S(1)} collective-permute-done((f32[2,64,4,64]{1,3,2,0:T(8,128)S(1)}, f32[2,64,4,64]{1,3,2,0:T(8,128)S(1)}, u32[]{:S(2)}, u32[]{:S(2)}) %collective-permute-start.6) | collective-permute-done | bytes 131104 | tf_op jit(solution)/shard_map/ppermute | solution.py:13
  218.2 4.8 %collective-permute-start.22 = (f32[2,64,4,64]{1,3,2,0:T(8,128)}, f32[2,64,4,64]{1,3,2,0:T(8,128)}, u32[]{:S(2)}, u32[]{:S(2)}) collective-permute-start(f32[2,64,4,64]{1,3,2,0:T(8,128)} %convolution_bitcast_fusion.4), channel_id=1, source_target_pairs={{0,232},{4,236},{8,240},{12,244},{16,248},{20,252},{24,0},{28,4},{... | collective-permute-start | bytes 393224 | tf_op jit(solution)/shard_map/ppermute | solution.py:13
  241.1 1.8 copy.185
  245.9 1.8 copy.190
  250.7 1.8 copy.195
  265.6 4.7 %collective-permute-start.2 = (f32[8,64,4,64]{1,3,2,0:T(8,128)S(1)}, f32[8,64,4,64]{1,3,2,0:T(8,128)S(1)}, u32[]{:S(2)}, u32[]{:S(2)}) collective-permute-start(f32[8,64,4,64]{1,3,2,0:T(8,128)S(1)} %convolution_bitcast_fusion), channel_id=1, source_target_pairs={{0,252},{4,0},{8,4},{12,8},{16,12},{20,16},{24,20},{28,24},{32,28}... | collective-permute-start | bytes 1572872 | tf_op jit(solution)/shard_map/ppermute | solution.py:13
  275.6 7.0 %collective-permute-done.2 = f32[8,64,4,64]{1,3,2,0:T(8,128)S(1)} collective-permute-done((f32[8,64,4,64]{1,3,2,0:T(8,128)S(1)}, f32[8,64,4,64]{1,3,2,0:T(8,128)S(1)}, u32[]{:S(2)}, u32[]{:S(2)}) %collective-permute-start.2) | collective-permute-done | bytes 524320 | tf_op jit(solution)/shard_map/ppermute | solution.py:13
  290.4 5.6 %multiply_reduce_fusion = f32[8,64,4,64]{1,3,2,0:T(8,128)S(1)} fusion(f32[9,8,64,4,64]{2,4,3,1,0:T(8,128)} %bitcast_dynamic-update-slice_fusion, f32[9,8,64,4]{2,3,1,0:T(4,128)S(1)} %get-tuple-element.21), kind=kLoop, calls=%fused_computation.31 | loop fusion | flops 2228224 | bytes 5316608 | tf_op jit(solution)/shard_map/reduce_sum | solution.py:29
  296.8 2.9 fusion.186
  299.7 88.6 %all-gather.6.cloned.1.call-done = f32[2048,1024]{1,0:T(8,128)} async-done(((f32[512,1024]{1,0:T(8,128)}), f32[2048,1024]{1,0:T(8,128)}) %all-gather.6.cloned.1.call-update) | async-done | bytes 8388624 | tf_op jit(solution)/shard_map/all_gather | solution.py:160
  388.4 6.0 %reduce_sum.164 = f32[512,1024]{1,0:T(8,128)} reduce(f32[4,512,1024]{2,1,0:T(8,128)} %bitcast.234, f32[]{:T(128)} %constant.54.clone.1), dimensions={0}, to_apply=%region_39.40 | reduce | flops 1572864 | bytes 10485764 | tf_op jit(solution)/shard_map/reduce_sum | solution.py:161
  394.3 2.2 fusion.77
  398.0 9.2 %convolution_convert_fusion = bf16[512,1024]{1,0:T(8,128)(2,1)} fusion(bf16[1024,1024]{1,0:T(8,128)(2,1)S(1)} %copy-done, bf16[512,1024]{1,0:T(8,128)(2,1)} %multiply_convert_fusion, bf16[1024,1024]{1,0:T(8,128)(2,1)} %param.16), kind=kOutput, calls=%fused_computation.54 | convolution fusion | flops 2182086656 | bytes 6291456 | tf_op jit(solution)/shard_map/dot_general | solution.py:170
  411.2 23.2 %reduce-scatter.2.cloned.1.call-done = bf16[512,256]{1,0:T(8,128)(2,1)} async-done(((bf16[512,1024]{1,0:T(8,128)(2,1)}), bf16[512,256]{1,0:T(8,128)(2,1)}) %reduce-scatter.2.cloned.1.call-update) | async-done | bytes 262160 | tf_op jit(solution)/shard_map/reduce_scatter | solution.py:169
  435.6 8.5 %all-reduce = (f32[512]{0:T(512)S(1)}, f32[512]{0:T(512)S(1)}) all-reduce(f32[512]{0:T(512)S(1)} %get-tuple-element.17, f32[512]{0:T(512)S(1)} %get-tuple-element.16), channel_id=1, replica_groups=mesh['req'=64,'tp'=4] {'tp'}, use_global_device_ids=true, to_apply=%region_46.47 | all-reduce | flops 1024 | bytes 8192 | tf_op jit(solution)/shard_map/psum | solution.py:176
  444.1 1.9 multiply_convert_fusion.1
  (355 shorter events, 132.2 us)
Async XLA Ops:
  7.2 390.8 %copy-start = (bf16[1024,1024]{1,0:T(8,128)(2,1)S(1)}, bf16[1024,1024]{1,0:T(8,128)(2,1)}, u32[]{:S(2)}) copy-start(bf16[1024,1024]{1,0:T(8,128)(2,1)} %param.17) | copy-start | bytes 6291460
  7.2 137.3 %all-gather.4.cloned.1.call-start = ((), (), s32[]{:S(2)}) async-start(), calls=%async_computation.1 | async-start | bytes 1310720 | tf_op jit(solution)/shard_map/all_gather | solution.py:102
  9.0 42.3 %collective-permute-start.7 = (bf16[2]{0:T(256)(128)(2,1)S(1)}, bf16[2]{0:T(256)(128)(2,1)S(1)}, u32[]{:S(2)}, u32[]{:S(2)}) collective-permute-start(bf16[2]{0:T(256)(128)(2,1)S(1)} %get-tuple-element.60), channel_id=1, source_target_pairs={{0,12},{4,16},{8,20},{12,24},{16,28},{20,32},{24,36},{28,40},{32,4... | collective-permute-start | bytes 20 | tf_op jit(solution)/shard_map/ppermute | solution.py:13
  9.9 44.2 %collective-permute-start.3 = (bf16[2]{0:T(256)(128)(2,1)S(1)}, bf16[2]{0:T(256)(128)(2,1)S(1)}, u32[]{:S(2)}, u32[]{:S(2)}) collective-permute-start(bf16[2]{0:T(256)(128)(2,1)S(1)} %get-tuple-element.60), channel_id=1, source_target_pairs={{0,8},{4,12},{8,16},{12,20},{16,24},{20,28},{24,32},{28,36},{32,40... | collective-permute-start | bytes 20 | tf_op jit(solution)/shard_map/ppermute | solution.py:13
  11.1 62.5 %collective-permute-start.15 = (bf16[2]{0:T(256)(128)(2,1)S(1)}, bf16[2]{0:T(256)(128)(2,1)S(1)}, u32[]{:S(2)}, u32[]{:S(2)}) collective-permute-start(bf16[2]{0:T(256)(128)(2,1)S(1)} %get-tuple-element.60), channel_id=1, source_target_pairs={{0,20},{4,24},{8,28},{12,32},{16,36},{20,40},{24,44},{28,48},{32,5... | collective-permute-start | bytes 20 | tf_op jit(solution)/shard_map/ppermute | solution.py:13
  15.4 60.7 %collective-permute-start.11 = (bf16[2]{0:T(256)(128)(2,1)S(1)}, bf16[2]{0:T(256)(128)(2,1)S(1)}, u32[]{:S(2)}, u32[]{:S(2)}) collective-permute-start(bf16[2]{0:T(256)(128)(2,1)S(1)} %get-tuple-element.60), channel_id=1, source_target_pairs={{0,16},{4,20},{8,24},{12,28},{16,32},{20,36},{24,40},{28,44},{32,4... | collective-permute-start | bytes 20 | tf_op jit(solution)/shard_map/ppermute | solution.py:13
  16.7 81.6 %collective-permute-start.23 = (bf16[2]{0:T(256)(128)(2,1)S(1)}, bf16[2]{0:T(256)(128)(2,1)S(1)}, u32[]{:S(2)}, u32[]{:S(2)}) collective-permute-start(bf16[2]{0:T(256)(128)(2,1)S(1)} %get-tuple-element.60), channel_id=1, source_target_pairs={{0,28},{4,32},{8,36},{12,40},{16,44},{20,48},{24,52},{28,56},{32,6... | collective-permute-start | bytes 20 | tf_op jit(solution)/shard_map/ppermute | solution.py:13
  17.4 371.0 %all-gather.6.cloned.1.call-start = ((), (), s32[]{:S(2)}) async-start(), calls=%async_computation.3 | async-start | bytes 10485760 | tf_op jit(solution)/shard_map/all_gather | solution.py:160
  51.3 49.1 %collective-permute-start.19 = (bf16[2]{0:T(256)(128)(2,1)S(1)}, bf16[2]{0:T(256)(128)(2,1)S(1)}, u32[]{:S(2)}, u32[]{:S(2)}) collective-permute-start(bf16[2]{0:T(256)(128)(2,1)S(1)} %get-tuple-element.60), channel_id=1, source_target_pairs={{0,24},{4,28},{8,32},{12,36},{16,40},{20,44},{24,48},{28,52},{32,5... | collective-permute-start | bytes 20 | tf_op jit(solution)/shard_map/ppermute | solution.py:13
  54.2 90.2 %collective-permute-start = (bf16[8,128]{1,0:T(8,128)(2,1)S(1)}, bf16[8,128]{1,0:T(8,128)(2,1)S(1)}, u32[]{:S(2)}, u32[]{:S(2)}) collective-permute-start(bf16[8,128]{1,0:T(8,128)(2,1)S(1)} %get-tuple-element.53), channel_id=1, source_target_pairs={{0,4},{4,8},{8,12},{12,16},{16,20},{20,24},{24,28},{28,32},{32,36}... | collective-permute-start | bytes 6152 | tf_op jit(solution)/shard_map/ppermute | solution.py:13
  73.6 65.1 %collective-permute-start.4 = (bf16[2,128]{1,0:T(2,128)(2,1)S(1)}, bf16[2,128]{1,0:T(2,128)(2,1)S(1)}, u32[]{:S(2)}, u32[]{:S(2)}) collective-permute-start(bf16[2,128]{1,0:T(2,128)(2,1)S(1)} %convert_element_type.237), channel_id=1, source_target_pairs={{0,8},{4,12},{8,16},{12,20},{16,24},{20,28},{24,32},{28,36},{32,40... | collective-permute-start | bytes 1544 | tf_op jit(solution)/shard_map/ppermute | solution.py:13
  76.1 62.7 %collective-permute-start.8 = (bf16[2,128]{1,0:T(2,128)(2,1)S(1)}, bf16[2,128]{1,0:T(2,128)(2,1)S(1)}, u32[]{:S(2)}, u32[]{:S(2)}) collective-permute-start(bf16[2,128]{1,0:T(2,128)(2,1)S(1)} %convert_element_type.241), channel_id=1, source_target_pairs={{0,12},{4,16},{8,20},{12,24},{16,28},{20,32},{24,36},{28,40},{32,4... | collective-permute-start | bytes 1544 | tf_op jit(solution)/shard_map/ppermute | solution.py:13
  98.3 42.3 %collective-permute-start.12 = (bf16[2,128]{1,0:T(2,128)(2,1)S(1)}, bf16[2,128]{1,0:T(2,128)(2,1)S(1)}, u32[]{:S(2)}, u32[]{:S(2)}) collective-permute-start(bf16[2,128]{1,0:T(2,128)(2,1)S(1)} %convert_element_type.245), channel_id=1, source_target_pairs={{0,16},{4,20},{8,24},{12,28},{16,32},{20,36},{24,40},{28,44},{32,4... | collective-permute-start | bytes 1544 | tf_op jit(solution)/shard_map/ppermute | solution.py:13
  100.3 40.3 %collective-permute-start.16 = (bf16[2,128]{1,0:T(2,128)(2,1)S(1)}, bf16[2,128]{1,0:T(2,128)(2,1)S(1)}, u32[]{:S(2)}, u32[]{:S(2)}) collective-permute-start(bf16[2,128]{1,0:T(2,128)(2,1)S(1)} %convert_element_type.249), channel_id=1, source_target_pairs={{0,20},{4,24},{8,28},{12,32},{16,36},{20,40},{24,44},{28,48},{32,5... | collective-permute-start | bytes 1544 | tf_op jit(solution)/shard_map/ppermute | solution.py:13
  138.7 5.7 %collective-permute-start.20 = (bf16[2,128]{1,0:T(2,128)(2,1)S(1)}, bf16[2,128]{1,0:T(2,128)(2,1)S(1)}, u32[]{:S(2)}, u32[]{:S(2)}) collective-permute-start(bf16[2,128]{1,0:T(2,128)(2,1)S(1)} %convert_element_type.253), channel_id=1, source_target_pairs={{0,24},{4,28},{8,32},{12,36},{16,40},{20,44},{24,48},{28,52},{32,5... | collective-permute-start | bytes 1544 | tf_op jit(solution)/shard_map/ppermute | solution.py:13
  138.7 5.6 %collective-permute-start.24 = (bf16[2,128]{1,0:T(2,128)(2,1)S(1)}, bf16[2,128]{1,0:T(2,128)(2,1)S(1)}, u32[]{:S(2)}, u32[]{:S(2)}) collective-permute-start(bf16[2,128]{1,0:T(2,128)(2,1)S(1)} %convert_element_type.257), channel_id=1, source_target_pairs={{0,28},{4,32},{8,36},{12,40},{16,44},{20,48},{24,52},{28,56},{32,6... | collective-permute-start | bytes 1544 | tf_op jit(solution)/shard_map/ppermute | solution.py:13
  153.2 17.6 %collective-permute-start.5 = (bf16[2,64,4,64]{3,1,2,0:T(8,128)(2,1)}, bf16[2,64,4,64]{3,1,2,0:T(8,128)(2,1)}, u32[]{:S(2)}, u32[]{:S(2)}) collective-permute-start(bf16[2,64,4,64]{3,1,2,0:T(8,128)(2,1)} %gather_fusion.2), channel_id=1, source_target_pairs={{0,8},{4,12},{8,16},{12,20},{16,24},{20,28},{24,32},{28,36},{32,40... | collective-permute-start | bytes 196616 | tf_op jit(solution)/shard_map/ppermute | solution.py:13
  154.6 18.1 %collective-permute-start.9 = (bf16[2,64,4,64]{3,1,2,0:T(8,128)(2,1)}, bf16[2,64,4,64]{3,1,2,0:T(8,128)(2,1)}, u32[]{:S(2)}, u32[]{:S(2)}) collective-permute-start(bf16[2,64,4,64]{3,1,2,0:T(8,128)(2,1)} %gather_fusion.2), channel_id=1, source_target_pairs={{0,12},{4,16},{8,20},{12,24},{16,28},{20,32},{24,36},{28,40},{32,4... | collective-permute-start | bytes 196616 | tf_op jit(solution)/shard_map/ppermute | solution.py:13
  154.7 22.1 %collective-permute-start.13 = (bf16[2,64,4,64]{3,1,2,0:T(8,128)(2,1)}, bf16[2,64,4,64]{3,1,2,0:T(8,128)(2,1)}, u32[]{:S(2)}, u32[]{:S(2)}) collective-permute-start(bf16[2,64,4,64]{3,1,2,0:T(8,128)(2,1)} %gather_fusion.2), channel_id=1, source_target_pairs={{0,16},{4,20},{8,24},{12,28},{16,32},{20,36},{24,40},{28,44},{32,4... | collective-permute-start | bytes 196616 | tf_op jit(solution)/shard_map/ppermute | solution.py:13
  156.9 25.3 %collective-permute-start.17 = (bf16[2,64,4,64]{3,1,2,0:T(8,128)(2,1)}, bf16[2,64,4,64]{3,1,2,0:T(8,128)(2,1)}, u32[]{:S(2)}, u32[]{:S(2)}) collective-permute-start(bf16[2,64,4,64]{3,1,2,0:T(8,128)(2,1)} %gather_fusion.2), channel_id=1, source_target_pairs={{0,20},{4,24},{8,28},{12,32},{16,36},{20,40},{24,44},{28,48},{32,5... | collective-permute-start | bytes 196616 | tf_op jit(solution)/shard_map/ppermute | solution.py:13
  158.4 29.3 %collective-permute-start.21 = (bf16[2,64,4,64]{3,1,2,0:T(8,128)(2,1)}, bf16[2,64,4,64]{3,1,2,0:T(8,128)(2,1)}, u32[]{:S(2)}, u32[]{:S(2)}) collective-permute-start(bf16[2,64,4,64]{3,1,2,0:T(8,128)(2,1)} %gather_fusion.2), channel_id=1, source_target_pairs={{0,24},{4,28},{8,32},{12,36},{16,40},{20,44},{24,48},{28,52},{32,5... | collective-permute-start | bytes 196616 | tf_op jit(solution)/shard_map/ppermute | solution.py:13
  170.8 18.4 %collective-permute-start.25 = (bf16[2,64,4,64]{3,1,2,0:T(8,128)(2,1)S(1)}, bf16[2,64,4,64]{3,1,2,0:T(8,128)(2,1)S(1)}, u32[]{:S(2)}, u32[]{:S(2)}) collective-permute-start(bf16[2,64,4,64]{3,1,2,0:T(8,128)(2,1)S(1)} %copy-done.31), channel_id=1, source_target_pairs={{0,28},{4,32},{8,36},{12,40},{16,44},{20,48},{24,52},{28,56},{32,6... | collective-permute-start | bytes 196616 | tf_op jit(solution)/shard_map/ppermute | solution.py:13
  172.8 20.0 %collective-permute-start.35 = (f32[2,4,64]{2,1,0:T(4,128)S(1)}, f32[2,4,64]{2,1,0:T(4,128)S(1)}, u32[]{:S(2)}, u32[]{:S(2)}) collective-permute-start(f32[2,4,64]{2,1,0:T(4,128)S(1)} %convert_reduce_fusion.8), channel_id=1, source_target_pairs={{0,248},{4,252},{8,0},{12,4},{16,8},{20,12},{24,16},{28,20},{32,24... | collective-permute-start | bytes 6152 | tf_op jit(solution)/shard_map/ppermute | solution.py:13
  176.7 16.7 %collective-permute-start.36 = (f32[2,4,64]{2,1,0:T(4,128)S(1)}, f32[2,4,64]{2,1,0:T(4,128)S(1)}, u32[]{:S(2)}, u32[]{:S(2)}) collective-permute-start(f32[2,4,64]{2,1,0:T(4,128)S(1)} %convert_reduce_fusion.7), channel_id=1, source_target_pairs={{0,244},{4,248},{8,252},{12,0},{16,4},{20,8},{24,12},{28,16},{32,2... | collective-permute-start | bytes 6152 | tf_op jit(solution)/shard_map/ppermute | solution.py:13
  180.8 21.5 %copy-start.20 = (bf16[2,128,1,256]{1,3,0,2:T(8,128)(2,1)S(1)}, bf16[2,128,1,256]{1,3,0,2:T(8,128)(2,1)}, u32[]{:S(2)}) copy-start(bf16[2,128,1,256]{1,3,0,2:T(8,128)(2,1)} %copy.193) | copy-start | bytes 393220
  181.9 27.9 %copy-start.19 = (bf16[2,128,1,256]{1,3,0,2:T(8,128)(2,1)S(1)}, bf16[2,128,1,256]{1,3,0,2:T(8,128)(2,1)}, u32[]{:S(2)}) copy-start(bf16[2,128,1,256]{1,3,0,2:T(8,128)(2,1)} %copy.198) | copy-start | bytes 393220
  182.1 15.5 %collective-permute-start.37 = (f32[2,4,64]{2,1,0:T(4,128)S(1)}, f32[2,4,64]{2,1,0:T(4,128)S(1)}, u32[]{:S(2)}, u32[]{:S(2)}) collective-permute-start(f32[2,4,64]{2,1,0:T(4,128)S(1)} %convert_reduce_fusion.6), channel_id=1, source_target_pairs={{0,240},{4,244},{8,248},{12,252},{16,0},{20,4},{24,8},{28,12},{32,... | collective-permute-start | bytes 6152 | tf_op jit(solution)/shard_map/ppermute | solution.py:13
  187.7 10.7 %collective-permute-start.38 = (f32[2,4,64]{2,1,0:T(4,128)S(1)}, f32[2,4,64]{2,1,0:T(4,128)S(1)}, u32[]{:S(2)}, u32[]{:S(2)}) collective-permute-start(f32[2,4,64]{2,1,0:T(4,128)S(1)} %convert_reduce_fusion.5), channel_id=1, source_target_pairs={{0,236},{4,240},{8,244},{12,248},{16,252},{20,0},{24,4},{28,8},{32... | collective-permute-start | bytes 6152 | tf_op jit(solution)/shard_map/ppermute | solution.py:13
  189.2 9.1 %collective-permute-start.39 = (f32[2,4,64]{2,1,0:T(4,128)S(1)}, f32[2,4,64]{2,1,0:T(4,128)S(1)}, u32[]{:S(2)}, u32[]{:S(2)}) collective-permute-start(f32[2,4,64]{2,1,0:T(4,128)S(1)} %convert_reduce_fusion.4), channel_id=1, source_target_pairs={{0,232},{4,236},{8,240},{12,244},{16,248},{20,252},{24,0},{28,4},{... | collective-permute-start | bytes 6152 | tf_op jit(solution)/shard_map/ppermute | solution.py:13
  192.8 11.3 %collective-permute-start.28 = (f32[2,4,64]{2,1,0:T(4,128)S(1)}, f32[2,4,64]{2,1,0:T(4,128)S(1)}, u32[]{:S(2)}, u32[]{:S(2)}) collective-permute-start(f32[2,4,64]{2,1,0:T(4,128)S(1)} %get-tuple-element.70), channel_id=1, source_target_pairs={{0,248},{4,252},{8,0},{12,4},{16,8},{20,12},{24,16},{28,20},{32,24... | collective-permute-start | bytes 6152 | tf_op jit(solution)/shard_map/ppermute | solution.py:13
  193.5 13.7 %collective-permute-start.29 = (f32[2,4,64]{2,1,0:T(4,128)S(1)}, f32[2,4,64]{2,1,0:T(4,128)S(1)}, u32[]{:S(2)}, u32[]{:S(2)}) collective-permute-start(f32[2,4,64]{2,1,0:T(4,128)S(1)} %get-tuple-element.72), channel_id=1, source_target_pairs={{0,244},{4,248},{8,252},{12,0},{16,4},{20,8},{24,12},{28,16},{32,2... | collective-permute-start | bytes 6152 | tf_op jit(solution)/shard_map/ppermute | solution.py:13
  197.6 9.6 %collective-permute-start.30 = (f32[2,4,64]{2,1,0:T(4,128)S(1)}, f32[2,4,64]{2,1,0:T(4,128)S(1)}, u32[]{:S(2)}, u32[]{:S(2)}) collective-permute-start(f32[2,4,64]{2,1,0:T(4,128)S(1)} %get-tuple-element.74), channel_id=1, source_target_pairs={{0,240},{4,244},{8,248},{12,252},{16,0},{20,4},{24,8},{28,12},{32,... | collective-permute-start | bytes 6152 | tf_op jit(solution)/shard_map/ppermute | solution.py:13
  198.4 10.2 %collective-permute-start.31 = (f32[2,4,64]{2,1,0:T(4,128)S(1)}, f32[2,4,64]{2,1,0:T(4,128)S(1)}, u32[]{:S(2)}, u32[]{:S(2)}) collective-permute-start(f32[2,4,64]{2,1,0:T(4,128)S(1)} %get-tuple-element.76), channel_id=1, source_target_pairs={{0,236},{4,240},{8,244},{12,248},{16,252},{20,0},{24,4},{28,8},{32... | collective-permute-start | bytes 6152 | tf_op jit(solution)/shard_map/ppermute | solution.py:13
  198.4 5.7 %collective-permute-start.40 = (f32[2,4,64]{2,1,0:T(4,128)S(1)}, f32[2,4,64]{2,1,0:T(4,128)S(1)}, u32[]{:S(2)}, u32[]{:S(2)}) collective-permute-start(f32[2,4,64]{2,1,0:T(4,128)S(1)} %convert_reduce_fusion.3), channel_id=1, source_target_pairs={{0,228},{4,232},{8,236},{12,240},{16,244},{20,248},{24,252},{28,0}... | collective-permute-start | bytes 6152 | tf_op jit(solution)/shard_map/ppermute | solution.py:13
  204.1 56.2 %collective-permute-start.1 = (bf16[8,64,4,64]{3,1,2,0:T(8,128)(2,1)}, bf16[8,64,4,64]{3,1,2,0:T(8,128)(2,1)}, u32[]{:S(2)}, u32[]{:S(2)}) collective-permute-start(bf16[8,64,4,64]{3,1,2,0:T(8,128)(2,1)} %copy.159), channel_id=1, source_target_pairs={{0,4},{4,8},{8,12},{12,16},{16,20},{20,24},{24,28},{28,32},{32,36}... | collective-permute-start | bytes 786440 | tf_op jit(solution)/shard_map/ppermute | solution.py:13
  204.1 6.7 %collective-permute-start.32 = (f32[2,4,64]{2,1,0:T(4,128)S(1)}, f32[2,4,64]{2,1,0:T(4,128)S(1)}, u32[]{:S(2)}, u32[]{:S(2)}) collective-permute-start(f32[2,4,64]{2,1,0:T(4,128)S(1)} %get-tuple-element.78), channel_id=1, source_target_pairs={{0,232},{4,236},{8,240},{12,244},{16,248},{20,252},{24,0},{28,4},{... | collective-permute-start | bytes 6152 | tf_op jit(solution)/shard_map/ppermute | solution.py:13
  207.2 5.9 %collective-permute-start.33 = (f32[2,4,64]{2,1,0:T(4,128)S(1)}, f32[2,4,64]{2,1,0:T(4,128)S(1)}, u32[]{:S(2)}, u32[]{:S(2)}) collective-permute-start(f32[2,4,64]{2,1,0:T(4,128)S(1)} %get-tuple-element.80), channel_id=1, source_target_pairs={{0,228},{4,232},{8,236},{12,240},{16,244},{20,248},{24,252},{28,0}... | collective-permute-start | bytes 6152 | tf_op jit(solution)/shard_map/ppermute | solution.py:13
  207.2 11.0 %collective-permute-start.6 = (f32[2,64,4,64]{1,3,2,0:T(8,128)S(1)}, f32[2,64,4,64]{1,3,2,0:T(8,128)S(1)}, u32[]{:S(2)}, u32[]{:S(2)}) collective-permute-start(f32[2,64,4,64]{1,3,2,0:T(8,128)S(1)} %convolution_bitcast_fusion.8), channel_id=1, source_target_pairs={{0,248},{4,252},{8,0},{12,4},{16,8},{20,12},{24,16},{28,20},{32,24... | collective-permute-start | bytes 393224 | tf_op jit(solution)/shard_map/ppermute | solution.py:13
  208.6 14.4 %collective-permute-start.10 = (f32[2,64,4,64]{1,3,2,0:T(8,128)S(1)}, f32[2,64,4,64]{1,3,2,0:T(8,128)S(1)}, u32[]{:S(2)}, u32[]{:S(2)}) collective-permute-start(f32[2,64,4,64]{1,3,2,0:T(8,128)S(1)} %convolution_bitcast_fusion.7), channel_id=1, source_target_pairs={{0,244},{4,248},{8,252},{12,0},{16,4},{20,8},{24,12},{28,16},{32,2... | collective-permute-start | bytes 393224 | tf_op jit(solution)/shard_map/ppermute | solution.py:13
  210.8 30.3 %collective-permute-start.14 = (f32[2,64,4,64]{1,3,2,0:T(8,128)}, f32[2,64,4,64]{1,3,2,0:T(8,128)}, u32[]{:S(2)}, u32[]{:S(2)}) collective-permute-start(f32[2,64,4,64]{1,3,2,0:T(8,128)} %convolution_bitcast_fusion.6), channel_id=1, source_target_pairs={{0,240},{4,244},{8,248},{12,252},{16,0},{20,4},{24,8},{28,12},{32,... | collective-permute-start | bytes 393224 | tf_op jit(solution)/shard_map/ppermute | solution.py:13
  213.1 32.8 %collective-permute-start.18 = (f32[2,64,4,64]{1,3,2,0:T(8,128)}, f32[2,64,4,64]{1,3,2,0:T(8,128)}, u32[]{:S(2)}, u32[]{:S(2)}) collective-permute-start(f32[2,64,4,64]{1,3,2,0:T(8,128)} %convolution_bitcast_fusion.5), channel_id=1, source_target_pairs={{0,236},{4,240},{8,244},{12,248},{16,252},{20,0},{24,4},{28,8},{32... | collective-permute-start | bytes 393224 | tf_op jit(solution)/shard_map/ppermute | solution.py:13
  218.2 32.5 %collective-permute-start.22 = (f32[2,64,4,64]{1,3,2,0:T(8,128)}, f32[2,64,4,64]{1,3,2,0:T(8,128)}, u32[]{:S(2)}, u32[]{:S(2)}) collective-permute-start(f32[2,64,4,64]{1,3,2,0:T(8,128)} %convolution_bitcast_fusion.4), channel_id=1, source_target_pairs={{0,232},{4,236},{8,240},{12,244},{16,248},{20,252},{24,0},{28,4},{... | collective-permute-start | bytes 393224 | tf_op jit(solution)/shard_map/ppermute | solution.py:13
  223.7 31.8 %collective-permute-start.26 = (f32[2,64,4,64]{1,3,2,0:T(8,128)}, f32[2,64,4,64]{1,3,2,0:T(8,128)}, u32[]{:S(2)}, u32[]{:S(2)}) collective-permute-start(f32[2,64,4,64]{1,3,2,0:T(8,128)} %convolution_bitcast_fusion.3), channel_id=1, source_target_pairs={{0,228},{4,232},{8,236},{12,240},{16,244},{20,248},{24,252},{28,0}... | collective-permute-start | bytes 393224 | tf_op jit(solution)/shard_map/ppermute | solution.py:13
  262.1 12.4 %collective-permute-start.27 = (f32[8,4,64]{2,1,0:T(4,128)S(1)}, f32[8,4,64]{2,1,0:T(4,128)S(1)}, u32[]{:S(2)}, u32[]{:S(2)}) collective-permute-start(f32[8,4,64]{2,1,0:T(4,128)S(1)} %get-tuple-element.68), channel_id=1, source_target_pairs={{0,252},{4,0},{8,4},{12,8},{16,12},{20,16},{24,20},{28,24},{32,28}... | collective-permute-start | bytes 24584 | tf_op jit(solution)/shard_map/ppermute | solution.py:13
  263.9 6.4 %collective-permute-start.34 = (f32[8,4,64]{2,1,0:T(4,128)S(1)}, f32[8,4,64]{2,1,0:T(4,128)S(1)}, u32[]{:S(2)}, u32[]{:S(2)}) collective-permute-start(f32[8,4,64]{2,1,0:T(4,128)S(1)} %convert_reduce_fusion), channel_id=1, source_target_pairs={{0,252},{4,0},{8,4},{12,8},{16,12},{20,16},{24,20},{28,24},{32,28}... | collective-permute-start | bytes 24584 | tf_op jit(solution)/shard_map/ppermute | solution.py:13
  265.6 17.0 %collective-permute-start.2 = (f32[8,64,4,64]{1,3,2,0:T(8,128)S(1)}, f32[8,64,4,64]{1,3,2,0:T(8,128)S(1)}, u32[]{:S(2)}, u32[]{:S(2)}) collective-permute-start(f32[8,64,4,64]{1,3,2,0:T(8,128)S(1)} %convolution_bitcast_fusion), channel_id=1, source_target_pairs={{0,252},{4,0},{8,4},{12,8},{16,12},{20,16},{24,20},{28,24},{32,28}... | collective-permute-start | bytes 1572872 | tf_op jit(solution)/shard_map/ppermute | solution.py:13
  299.6 134.8 %reduce-scatter.2.cloned.1.call-start = ((), (), s32[]{:S(2)}) async-start(), calls=%async_computation.2 | async-start | bytes 1310720 | tf_op jit(solution)/shard_map/reduce_scatter | solution.py:169
  407.2 27.2 %copy-start.9 = (bf16[512,1024]{1,0:T(8,128)(2,1)S(1)}, bf16[512,1024]{1,0:T(8,128)(2,1)}, u32[]{:S(2)}) copy-start(bf16[512,1024]{1,0:T(8,128)(2,1)} %multiply_convert_fusion) | copy-start | bytes 3145732
  (44 other events, 319.0 us)
Sparse Core Ops, SparseCore 0:
  17.5 30.9 all-gather.3
  299.8 88.5 all-gather.5
  407.3 27.0 reduce-scatter.1
